TPU v7x, 256 devices: a whole 4x4x8 slice. The times are simulated.
256 devices in a mesh: region: 8 (over x, core), sub: 32 (over z, y).
Axes of the slice: x: 4, y: 4, z: 8, core: 2. Of those that a mesh axis runs over, the one named last changes fastest.
Arguments:
- query_rows: bfloat16 [131072, 512], P(('region', 'sub')), parts along dimension 0, may hold values from -8 to 8
- key_rows: bfloat16 [131072, 512], P(('region', 'sub')), parts along dimension 0, may hold values from -8 to 8
- value_rows: bfloat16 [131072, 512], P(('region', 'sub')), parts along dimension 0, may hold values from -6 to 6
- grad_out: bfloat16 [131072, 512], P(('region', 'sub')), parts along dimension 0, may hold values from -6 to 6
- partner_balls: int32 [1024, 4], P('region'), parts along dimension 0, may hold values from 0 to 127, as said below
Outputs:
- grad_queries: bfloat16 [131072, 512], P(('region', 'sub')), parts along dimension 0
- grad_keys: bfloat16 [131072, 512], P(('region', 'sub')), parts along dimension 0
- grad_values: bfloat16 [131072, 512], P(('region', 'sub')), parts along dimension 0
There are 8 independent parts, one for each index of `region`. A program takes and returns all parts, laid end to end along the dimension named above; each array names one. Nothing has to cross between parts.
Inputs may be any that keep to these rules, and one draw needn't show every extreme that they name: `partner_balls`: row b lists 4 distinct balls. Every listed ball lies in a subregion whose index differs from the index of b's subregion in exactly one bit; for every subregion s and each of the 5 subregions that differ from s in one bit, the balls of s together name exactly 1 distinct balls of that subregion.
All inputs are finite; a program needn't handle non-finite values.
Results may differ from a plain program's by a relative error of at most 0.0086.
Values may be sent and summed in bfloat16 or wider, within the bound.
A program may use at most 128 MiB of HBM per device.

v0:
```python
import functools

import jax
import jax.numpy as jnp
from jax import lax
from jax.experimental import pallas as pl
from jax.experimental.pallas import tpu as pltpu
from jax.sharding import PartitionSpec as P

HEADS = 8
HDIM = 64
BALL = 128
BALLS = 4
BITS = 5
ROWS = BALL * BALLS
WIDTH = HEADS * HDIM
SLAB = 2 * HDIM
PAIRS = HEADS // 2
FAR = BITS * BALL
KEYS = ROWS + FAR
QB = 256
UNITS = 2 * ROWS // QB
MESH = pl.DeviceIdType.MESH
SENDS = (4, 3, 2, 1, 0)
NN = (((1,), (0,)), ((), ()))
NT = (((1,), (1,)), ((), ()))


def mm(a, b, dims):
    return lax.dot_general(a, b, dims, preferred_element_type=jnp.float32)


def kernel(
    pb_ref, q_ref, k_ref, v_ref, g_ref, oq_ref, ok_ref, ov_ref,
    sbuf, rbuf, bsend, brecv, bias, rq, rg, kt, s_scr, dp_scr, p_scr, ds_scr,
    dqt, gk, gv, s_sem, r_sem, bs_sem, br_sem,
):
    region = lax.axis_index("region")
    me = lax.axis_index("sub")
    peers = [jnp.bitwise_xor(me, 1 << b) for b in range(BITS)]
    barrier = pltpu.get_barrier_semaphore()
    for peer in peers:
        pl.semaphore_signal(
            barrier, inc=1, device_id=(region, peer), device_id_type=MESH
        )

    named = []
    for b in range(BITS):
        ball = jnp.int32(0)
        for r in range(BALLS):
            for c in range(BALLS):
                entry = pb_ref[peers[b] * BALLS + r, c]
                ball = jnp.where(entry // BALLS == me, entry % BALLS, ball)
        named.append(ball)
    for b in SENDS:
        kb = k_ref[named[b]]
        vb = v_ref[named[b]]
        for p in range(PAIRS):
            sbuf[p, 0, b] = kb[:, p * SLAB : (p + 1) * SLAB]
            sbuf[p, 1, b] = vb[:, p * SLAB : (p + 1) * SLAB]

    def ahead(p, b):
        return pltpu.make_async_remote_copy(
            src_ref=sbuf.at[p, :, b],
            dst_ref=rbuf.at[p, :, b],
            send_sem=s_sem.at[p, b],
            recv_sem=r_sem.at[p, b],
            device_id=(region, peers[b]),
            device_id_type=MESH,
        )

    def back(p, b):
        return pltpu.make_async_remote_copy(
            src_ref=bsend.at[p, :, b],
            dst_ref=brecv.at[p, :, b],
            send_sem=bs_sem.at[p, b],
            recv_sem=br_sem.at[p, b],
            device_id=(region, peers[b]),
            device_id_type=MESH,
        )

    pl.semaphore_wait(barrier, BITS)

    @pl.loop(0, PAIRS)
    def _(p):
        for b in SENDS:
            ahead(p, b).start()

    for b in range(BITS):
        for r in range(BALLS):
            seen = jnp.float32(-1e30)
            for c in range(BALLS):
                entry = pb_ref[me * BALLS + r, c]
                seen = jnp.where(entry // BALLS == peers[b], jnp.float32(0), seen)
            bias[b, :, r * BALL : (r + 1) * BALL] = jnp.full((8, BALL), seen)

    lane = lax.broadcasted_iota(jnp.int32, (ROWS, SLAB), 1)

    @pl.loop(0, PAIRS)
    def _(p):
        cols = pl.ds(pl.multiple_of(p * SLAB, SLAB), SLAB)
        q = q_ref[:, cols] * jnp.bfloat16(HDIM**-0.5)
        g = g_ref[:, cols]
        zero = jnp.zeros_like(q)
        for hh in range(2):
            mine = (lane // HDIM) == hh
            rq[hh * ROWS : (hh + 1) * ROWS] = jnp.where(mine, q, zero)
            rg[hh * ROWS : (hh + 1) * ROWS] = jnp.where(mine, g, zero)
        for i in range(BALLS):
            kt[:, i * BALL : (i + 1) * BALL] = k_ref[i, :, cols].T
        for b in range(BITS):
            ahead(p, b).wait_recv()
        for b in range(BITS):
            kt[:, ROWS + b * BALL : ROWS + (b + 1) * BALL] = rbuf[p, 0, b].T

        def keys_of(i):
            return k_ref[i, :, cols] if i < BALLS else rbuf[p, 0, i - BALLS]

        def values_of(i):
            return v_ref[i, :, cols] if i < BALLS else rbuf[p, 1, i - BALLS]

        for u in range(UNITS):
            hh, qb = u // (ROWS // QB), u % (ROWS // QB)
            qu = rq[u * QB : (u + 1) * QB]
            gu = rg[u * QB : (u + 1) * QB]
            top = None
            for i in range(BALLS + BITS):
                s = mm(keys_of(i), qu, NT)
                if i >= BALLS:
                    s = s + bias[i - BALLS, 0:1, qb * QB : (qb + 1) * QB]
                s_scr[i] = s
                m = jnp.max(s.reshape(BALL // 8, 8, QB), axis=0)
                top = m if top is None else jnp.maximum(top, m)
            top = jnp.max(top, axis=0, keepdims=True)
            total = jnp.zeros((8, QB), jnp.float32)
            mean = jnp.zeros((8, QB), jnp.float32)
            for i in range(BALLS + BITS):
                dp = mm(values_of(i), gu, NT)
                e = jnp.exp(s_scr[i] - top)
                s_scr[i] = e
                dp_scr[i] = dp
                total = total + jnp.sum(e.reshape(BALL // 8, 8, QB), axis=0)
                mean = mean + jnp.sum((e * dp).reshape(BALL // 8, 8, QB), axis=0)
            scale = 1.0 / jnp.sum(total, axis=0, keepdims=True)
            delta = jnp.sum(mean, axis=0, keepdims=True) * scale
            at = slice(u * QB, (u + 1) * QB)
            for i in range(BALLS + BITS):
                pr = s_scr[i] * scale
                ds = pr * (dp_scr[i] - delta)
                p_scr[i * BALL : (i + 1) * BALL, at] = pr.astype(jnp.bfloat16)
                ds_scr[i * BALL : (i + 1) * BALL, at] = ds.astype(jnp.bfloat16)

        for b in range(BITS):
            at = slice(ROWS + b * BALL, ROWS + (b + 1) * BALL)
            bsend[p, 0, b] = mm(ds_scr[at], rq[...], NN).astype(jnp.bfloat16)
            bsend[p, 1, b] = mm(p_scr[at], rg[...], NN).astype(jnp.bfloat16)
        for b in SENDS:
            back(p, b).start()
        for i in range(BALLS):
            at = slice(i * BALL, (i + 1) * BALL)
            gk[p, i] = mm(ds_scr[at], rq[...], NN)
            gv[p, i] = mm(p_scr[at], rg[...], NN)
        for u in range(UNITS):
            hh, qb = u // (ROWS // QB), u % (ROWS // QB)
            dqt[hh * HDIM : (hh + 1) * HDIM, qb * QB : (qb + 1) * QB] = mm(
                kt[hh * HDIM : (hh + 1) * HDIM], ds_scr[:, u * QB : (u + 1) * QB], NN
            )
        oq_ref[:, cols] = (dqt[...].T * HDIM**-0.5).astype(jnp.bfloat16)

    share = [
        [jnp.where(named[b] == i, jnp.float32(1), jnp.float32(0)) for b in range(BITS)]
        for i in range(BALLS)
    ]

    @pl.loop(0, PAIRS)
    def _(p):
        cols = pl.ds(pl.multiple_of(p * SLAB, SLAB), SLAB)
        for b in range(BITS):
            back(p, b).wait_recv()
        for i in range(BALLS):
            ak, av = gk[p, i], gv[p, i]
            for b in range(BITS):
                ak = ak + share[i][b] * brecv[p, 0, b].astype(jnp.float32)
                av = av + share[i][b] * brecv[p, 1, b].astype(jnp.float32)
            ok_ref[i, :, cols] = ak.astype(jnp.bfloat16)
            ov_ref[i, :, cols] = av.astype(jnp.bfloat16)

    @pl.loop(0, PAIRS)
    def _(p):
        for b in range(BITS):
            ahead(p, b).wait_send()
            back(p, b).wait_send()


def body(query_rows, key_rows, value_rows, grad_out, partner_balls):
    vmem = pl.BlockSpec(memory_space=pltpu.VMEM)
    rows = jax.ShapeDtypeStruct((ROWS, WIDTH), jnp.bfloat16)
    balls = jax.ShapeDtypeStruct((BALLS, BALL, WIDTH), jnp.bfloat16)
    link = pltpu.VMEM((PAIRS, 2, BITS, BALL, SLAB), jnp.bfloat16)
    sem = pltpu.SemaphoreType.DMA((PAIRS, BITS))
    near = pltpu.VMEM((PAIRS, BALLS, BALL, SLAB), jnp.float32)
    grad_queries, grad_keys, grad_values = pl.pallas_call(
        kernel,
        out_shape=(rows, balls, balls),
        in_specs=[pl.BlockSpec(memory_space=pltpu.SMEM)] + [vmem] * 4,
        out_specs=(vmem, vmem, vmem),
        scratch_shapes=[
            link, link, link, link,
            pltpu.VMEM((BITS, 8, ROWS), jnp.float32),
            pltpu.VMEM((2 * ROWS, SLAB), jnp.bfloat16),
            pltpu.VMEM((2 * ROWS, SLAB), jnp.bfloat16),
            pltpu.VMEM((SLAB, KEYS), jnp.bfloat16),
            pltpu.VMEM((BALLS + BITS, BALL, QB), jnp.float32),
            pltpu.VMEM((BALLS + BITS, BALL, QB), jnp.float32),
            pltpu.VMEM((KEYS, 2 * ROWS), jnp.bfloat16),
            pltpu.VMEM((KEYS, 2 * ROWS), jnp.bfloat16),
            pltpu.VMEM((SLAB, ROWS), jnp.float32),
            near, near,
            sem, sem, sem, sem,
        ],
        compiler_params=pltpu.CompilerParams(
            collective_id=0, has_side_effects=True, vmem_limit_bytes=48 << 20
        ),
    )(
        partner_balls,
        query_rows,
        key_rows.reshape(BALLS, BALL, WIDTH),
        value_rows.reshape(BALLS, BALL, WIDTH),
        grad_out,
    )
    return (
        grad_queries,
        grad_keys.reshape(ROWS, WIDTH),
        grad_values.reshape(ROWS, WIDTH),
    )


def solution(mesh):
    rows = P(("region", "sub"), None)
    return jax.shard_map(
        body,
        mesh=mesh,
        in_specs=(rows, rows, rows, rows, P("region", None)),
        out_specs=(rows, rows, rows),
        check_vma=False,
    )
```

profile of v0, /device:TPU:8, one launch (start us, length us, event | category | flops | bytes accessed | tf_op | source)
XLA Modules:
  0.0 64.7 jit_solution(7562516574198916221)
XLA Ops:
  0.6 0.0 copy-start.4
  0.6 0.7 %copy-done.4 = s32[128,4]{0,1:T(4,128)S(1)} copy-done((s32[128,4]{0,1:T(4,128)S(1)}, s32[128,4]{0,1:T(4,128)}, u32[]{:S(2)}) %copy-start.4) | copy-done | bytes 2072
  1.3 0.1 copy.8.pb_ref
  1.4 0.0 copy-start
  1.4 1.0 %copy-done = bf16[512,512]{1,0:T(8,128)(2,1)S(1)} copy-done((bf16[512,512]{1,0:T(8,128)(2,1)S(1)}, bf16[512,512]{1,0:T(8,128)(2,1)}, u32[]{:S(2)}) %copy-start) | copy-done | bytes 524312
  2.5 0.0 copy-start.1
  2.5 1.0 %copy-done.1 = bf16[512,512]{1,0:T(8,128)(2,1)S(1)} copy-done((bf16[512,512]{1,0:T(8,128)(2,1)S(1)}, bf16[512,512]{1,0:T(8,128)(2,1)}, u32[]{:S(2)}) %copy-start.1) | copy-done | bytes 524312
  3.5 0.0 copy-start.2
  3.5 1.0 %copy-done.2 = bf16[512,512]{1,0:T(8,128)(2,1)S(1)} copy-done((bf16[512,512]{1,0:T(8,128)(2,1)S(1)}, bf16[512,512]{1,0:T(8,128)(2,1)}, u32[]{:S(2)}) %copy-start.2) | copy-done | bytes 524312
  4.6 0.0 copy-start.3
  4.6 1.0 %copy-done.3 = bf16[512,512]{1,0:T(8,128)(2,1)S(1)} copy-done((bf16[512,512]{1,0:T(8,128)(2,1)S(1)}, bf16[512,512]{1,0:T(8,128)(2,1)}, u32[]{:S(2)}) %copy-start.3) | copy-done | bytes 524312
  5.6 56.8 %shard_map.76 = (bf16[512,512]{1,0:T(8,128)(2,1)S(1)}, bf16[4,128,512]{2,1,0:T(8,128)(2,1)S(1)}, bf16[4,128,512]{2,1,0:T(8,128)(2,1)S(1)}) custom-call(s32[128,4]{1,0:T(8,128)S(1)} %copy.8.pb_ref, bf16[512,512]{1,0:T(8,128)(2,1)S(1)} %copy-done, bf16[4,128,512]{2,1,0:T(8,128)(2,1)S(1)} %bitcast.6, bf16[4,128,512]{2,1,0:T(8,128)(2,1)S(1)} %bitcast.7, ...), custom_call_target="tpu_custom_call" | custom-call | tf_op jit(solution)/shard_map/pallas_call | solution.py:202
  62.4 0.8 %copy.12 = bf16[512,512]{1,0:T(8,128)(2,1)} copy(bf16[512,512]{1,0:T(8,128)(2,1)S(1)} %get-tuple-element.12) | data formatting | bytes 1048576
  63.2 0.8 %copy.13 = bf16[512,512]{1,0:T(8,128)(2,1)} copy(bf16[512,512]{1,0:T(8,128)(2,1)S(1)} %bitcast.5) | data formatting | bytes 1048576
  63.9 0.8 %copy.14 = bf16[512,512]{1,0:T(8,128)(2,1)} copy(bf16[512,512]{1,0:T(8,128)(2,1)S(1)} %bitcast.4) | data formatting | bytes 1048576
Async XLA Ops:
  0.6 0.7 %copy-start.4 = (s32[128,4]{0,1:T(4,128)S(1)}, s32[128,4]{0,1:T(4,128)}, u32[]{:S(2)}) copy-start(s32[128,4]{0,1:T(4,128)} %param.9) | copy-start | bytes 6148
  1.4 1.0 %copy-start = (bf16[512,512]{1,0:T(8,128)(2,1)S(1)}, bf16[512,512]{1,0:T(8,128)(2,1)}, u32[]{:S(2)}) copy-start(bf16[512,512]{1,0:T(8,128)(2,1)} %q_ref.1) | copy-start | bytes 1572868
  2.5 1.0 %copy-start.1 = (bf16[512,512]{1,0:T(8,128)(2,1)S(1)}, bf16[512,512]{1,0:T(8,128)(2,1)}, u32[]{:S(2)}) copy-start(bf16[512,512]{1,0:T(8,128)(2,1)} %param.6) | copy-start | bytes 1572868
  3.5 1.0 %copy-start.2 = (bf16[512,512]{1,0:T(8,128)(2,1)S(1)}, bf16[512,512]{1,0:T(8,128)(2,1)}, u32[]{:S(2)}) copy-start(bf16[512,512]{1,0:T(8,128)(2,1)} %param.7) | copy-start | bytes 1572868
  4.6 1.0 %copy-start.3 = (bf16[512,512]{1,0:T(8,128)(2,1)S(1)}, bf16[512,512]{1,0:T(8,128)(2,1)}, u32[]{:S(2)}) copy-start(bf16[512,512]{1,0:T(8,128)(2,1)} %g_ref.1) | copy-start | bytes 1572868
where the time goes:
time: 65 us; the launch traced here: 64.7 us
  Pallas kernels  56.8 us (87%)
  local copies, waits for them, and re-layouts  7.33 us (11%)
  between operations  0.66 us (1%)
    pallas_call x1, Pallas kernels, body(): pl.pallas_call(kernel, out_shape=(rows, balls, balls), in_specs=[pl.Block...  56.8 us
    unnamed x14, local copies, waits for them, and re-layouts  7.33 us

commit v1 on v0

--- a/solution.py
+++ b/solution.py
@@ -31,10 +31,25 @@
 
 
 def kernel(
-    pb_ref, q_ref, k_ref, v_ref, g_ref, oq_ref, ok_ref, ov_ref,
-    sbuf, rbuf, bsend, brecv, bias, rq, rg, kt, s_scr, dp_scr, p_scr, ds_scr,
+    pb_hbm, q_hbm, k_hbm, v_hbm, g_hbm, out,
+    pb_ref, q_ref, k_ref, v_ref, g_ref, sbuf, rbuf, bsend, brecv, bias, rq, rg, kt, s_scr, dp_scr, p_scr, ds_scr,
     dqt, gk, gv, s_sem, r_sem, bs_sem, br_sem,
+    pb_sem, in_sem,
 ):
+    table = pltpu.make_async_copy(pb_hbm, pb_ref, pb_sem)
+    table.start()
+    fetch = [
+        [
+            pltpu.make_async_copy(src.at[i], dst.at[i], in_sem.at[n, i])
+            for i in range(BALLS)
+        ]
+        for n, (src, dst) in enumerate(
+            ((k_hbm, k_ref), (v_hbm, v_ref), (q_hbm, q_ref), (g_hbm, g_ref))
+        )
+    ]
+    for copies in fetch:
+        for copy in copies:
+            copy.start()
     region = lax.axis_index("region")
     me = lax.axis_index("sub")
     peers = [jnp.bitwise_xor(me, 1 << b) for b in range(BITS)]
@@ -44,14 +59,18 @@
             barrier, inc=1, device_id=(region, peer), device_id_type=MESH
         )
 
+    table.wait()
     named = []
     for b in range(BITS):
         ball = jnp.int32(0)
         for r in range(BALLS):
             for c in range(BALLS):
-                entry = pb_ref[peers[b] * BALLS + r, c]
+                entry = pb_ref[c, peers[b] * BALLS + r]
                 ball = jnp.where(entry // BALLS == me, entry % BALLS, ball)
         named.append(ball)
+    for copies in fetch[:2]:
+        for copy in copies:
+            copy.wait()
     for b in SENDS:
         kb = k_ref[named[b]]
         vb = v_ref[named[b]]
@@ -90,17 +109,20 @@
         for r in range(BALLS):
             seen = jnp.float32(-1e30)
             for c in range(BALLS):
-                entry = pb_ref[me * BALLS + r, c]
+                entry = pb_ref[c, me * BALLS + r]
                 seen = jnp.where(entry // BALLS == peers[b], jnp.float32(0), seen)
             bias[b, :, r * BALL : (r + 1) * BALL] = jnp.full((8, BALL), seen)
 
+    for copies in fetch[2:]:
+        for copy in copies:
+            copy.wait()
     lane = lax.broadcasted_iota(jnp.int32, (ROWS, SLAB), 1)
 
     @pl.loop(0, PAIRS)
     def _(p):
         cols = pl.ds(pl.multiple_of(p * SLAB, SLAB), SLAB)
-        q = q_ref[:, cols] * jnp.bfloat16(HDIM**-0.5)
-        g = g_ref[:, cols]
+        q = q_ref[:, :, cols].reshape(ROWS, SLAB) * jnp.bfloat16(HDIM**-0.5)
+        g = g_ref[:, :, cols].reshape(ROWS, SLAB)
         zero = jnp.zeros_like(q)
         for hh in range(2):
             mine = (lane // HDIM) == hh
@@ -165,7 +187,9 @@
             dqt[hh * HDIM : (hh + 1) * HDIM, qb * QB : (qb + 1) * QB] = mm(
                 kt[hh * HDIM : (hh + 1) * HDIM], ds_scr[:, u * QB : (u + 1) * QB], NN
             )
-        oq_ref[:, cols] = (dqt[...].T * HDIM**-0.5).astype(jnp.bfloat16)
+        for i in range(BALLS):
+            dq = dqt[:, i * BALL : (i + 1) * BALL].T * HDIM**-0.5
+            out[0, i, :, cols] = dq.astype(jnp.bfloat16)
 
     share = [
         [jnp.where(named[b] == i, jnp.float32(1), jnp.float32(0)) for b in range(BITS)]
@@ -182,8 +206,8 @@
             for b in range(BITS):
                 ak = ak + share[i][b] * brecv[p, 0, b].astype(jnp.float32)
                 av = av + share[i][b] * brecv[p, 1, b].astype(jnp.float32)
-            ok_ref[i, :, cols] = ak.astype(jnp.bfloat16)
-            ov_ref[i, :, cols] = av.astype(jnp.bfloat16)
+            out[1, i, :, cols] = ak.astype(jnp.bfloat16)
+            out[2, i, :, cols] = av.astype(jnp.bfloat16)
 
     @pl.loop(0, PAIRS)
     def _(p):
@@ -192,19 +216,34 @@
             back(p, b).wait_send()
 
 
+def deliver(grads, oq_ref, ok_ref, ov_ref, sem):
+    copies = [
+        pltpu.make_async_copy(grads.at[n, i], dst.at[i], sem.at[n, i])
+        for n, dst in enumerate((oq_ref, ok_ref, ov_ref))
+        for i in range(BALLS)
+    ]
+    for copy in copies:
+        copy.start()
+    for copy in copies:
+        copy.wait()
+
+
 def body(query_rows, key_rows, value_rows, grad_out, partner_balls):
     vmem = pl.BlockSpec(memory_space=pltpu.VMEM)
-    rows = jax.ShapeDtypeStruct((ROWS, WIDTH), jnp.bfloat16)
+    hbm = pl.BlockSpec(memory_space=pltpu.HBM)
     balls = jax.ShapeDtypeStruct((BALLS, BALL, WIDTH), jnp.bfloat16)
     link = pltpu.VMEM((PAIRS, 2, BITS, BALL, SLAB), jnp.bfloat16)
     sem = pltpu.SemaphoreType.DMA((PAIRS, BITS))
     near = pltpu.VMEM((PAIRS, BALLS, BALL, SLAB), jnp.float32)
-    grad_queries, grad_keys, grad_values = pl.pallas_call(
+    rows = pltpu.VMEM((BALLS, BALL, WIDTH), jnp.bfloat16)
+    grads = pl.pallas_call(
         kernel,
-        out_shape=(rows, balls, balls),
-        in_specs=[pl.BlockSpec(memory_space=pltpu.SMEM)] + [vmem] * 4,
-        out_specs=(vmem, vmem, vmem),
+        out_shape=pltpu.VMEM((3, BALLS, BALL, WIDTH), jnp.bfloat16),
+        in_specs=[hbm] * 5,
+        out_specs=vmem,
         scratch_shapes=[
+            pltpu.SMEM((BALLS, BALLS * 32), jnp.int32),
+            rows, rows, rows, rows,
             link, link, link, link,
             pltpu.VMEM((BITS, 8, ROWS), jnp.float32),
             pltpu.VMEM((2 * ROWS, SLAB), jnp.bfloat16),
@@ -217,22 +256,30 @@
             pltpu.VMEM((SLAB, ROWS), jnp.float32),
             near, near,
             sem, sem, sem, sem,
+            pltpu.SemaphoreType.DMA,
+            pltpu.SemaphoreType.DMA((4, BALLS)),
         ],
         compiler_params=pltpu.CompilerParams(
-            collective_id=0, has_side_effects=True, vmem_limit_bytes=48 << 20
+            collective_id=0, has_side_effects=True, vmem_limit_bytes=40 << 20
         ),
     )(
-        partner_balls,
-        query_rows,
-        key_rows.reshape(BALLS, BALL, WIDTH),
-        value_rows.reshape(BALLS, BALL, WIDTH),
-        grad_out,
+        pltpu.with_memory_space_constraint(partner_balls.T, pltpu.HBM),
+        *(
+            pltpu.with_memory_space_constraint(
+                x.reshape(BALLS, BALL, WIDTH), pltpu.HBM
+            )
+            for x in (query_rows, key_rows, value_rows, grad_out)
+        ),
     )
-    return (
-        grad_queries,
-        grad_keys.reshape(ROWS, WIDTH),
-        grad_values.reshape(ROWS, WIDTH),
-    )
+    grads = pl.pallas_call(
+        deliver,
+        out_shape=(balls, balls, balls),
+        in_specs=[vmem],
+        out_specs=(hbm, hbm, hbm),
+        scratch_shapes=[pltpu.SemaphoreType.DMA((3, BALLS))],
+        compiler_params=pltpu.CompilerParams(vmem_limit_bytes=8 << 20),
+    )(pltpu.with_memory_space_constraint(grads, pltpu.VMEM))
+    return tuple(x.reshape(ROWS, WIDTH) for x in grads)
 
 
 def solution(mesh):

time: 65 us -> 57.4 us (0.88)
  local copies, waits for them, and re-layouts: 7.33 us -> 0 us
    unnamed x14 -> x0, local copies, waits for them, and re-layouts: 7.33 us -> none
    pallas_call x1 -> x2, Pallas kernels: 56.8 us -> 56.7 us  [the longest x1 55.5 us: body(): pl.pallas_call(kernel, out_shape=pltpu.VMEM((3, BALLS, BALL, WIDTH), jnp....]
where the time goes in v1:
time: 57.4 us; the launch traced here: 57.3 us
  Pallas kernels  56.7 us (99%)
  between operations  0.64 us (1%)
    pallas_call x1, Pallas kernels, body(): pl.pallas_call(kernel, out_shape=pltpu.VMEM((3, BALLS, BALL, WIDTH), jnp....  55.5 us
    pallas_call x1, Pallas kernels, body(): pl.pallas_call(deliver, out_shape=(balls, balls, balls), in_specs=[vmem],...  1.23 us

profile of v1, /device:TPU:8, one launch (start us, length us, event | category | flops | bytes accessed | tf_op | source)
XLA Modules:
  0.0 57.3 jit_solution(8031198799042324717)
XLA Ops:
  0.6 55.5 %shard_map.76.grads = bf16[3,4,128,512]{3,2,1,0:T(8,128)(2,1)S(1)} custom-call(s32[4,128]{1,0:T(4,128)} %bitcast.12, bf16[4,128,512]{2,1,0:T(8,128)(2,1)} %bitcast.8, bf16[4,128,512]{2,1,0:T(8,128)(2,1)} %bitcast.9, bf16[4,128,512]{2,1,0:T(8,128)(2,1)} %bitcast.10, bf16[4,128,512]{2,1,0:T(8,128)(2,1)} %bitcast.11), custom_call_target="tpu_custom_call" | custom-call | tf_op jit(solution)/shard_map/pallas_call | solution.py:239
  56.1 1.2 %shard_map.77 = (bf16[4,128,512]{2,1,0:T(8,128)(2,1)}, bf16[4,128,512]{2,1,0:T(8,128)(2,1)}, bf16[4,128,512]{2,1,0:T(8,128)(2,1)}) custom-call(bf16[3,4,128,512]{3,2,1,0:T(8,128)(2,1)S(1)} %shard_map.76.grads), custom_call_target="tpu_custom_call" | custom-call | tf_op jit(solution)/shard_map/pallas_call | solution.py:274

commit v2 on v1

--- a/solution.py
+++ b/solution.py
@@ -47,7 +47,7 @@
             ((k_hbm, k_ref), (v_hbm, v_ref), (q_hbm, q_ref), (g_hbm, g_ref))
         )
     ]
-    for copies in fetch:
+    for copies in fetch[:2]:
         for copy in copies:
             copy.start()
     region = lax.axis_index("region")
@@ -71,6 +71,9 @@
     for copies in fetch[:2]:
         for copy in copies:
             copy.wait()
+    for copies in fetch[2:]:
+        for copy in copies:
+            copy.start()
     for b in SENDS:
         kb = k_ref[named[b]]
         vb = v_ref[named[b]]
@@ -141,36 +144,42 @@
         def values_of(i):
             return v_ref[i, :, cols] if i < BALLS else rbuf[p, 1, i - BALLS]
 
-        for u in range(UNITS):
+        @pl.loop(0, UNITS)
+        def _(u):
             hh, qb = u // (ROWS // QB), u % (ROWS // QB)
-            qu = rq[u * QB : (u + 1) * QB]
-            gu = rg[u * QB : (u + 1) * QB]
+            at = pl.ds(pl.multiple_of(u * QB, QB), QB)
+            some = pl.ds(pl.multiple_of(qb * QB, QB), QB)
+            head = pl.ds(pl.multiple_of(hh * HDIM, HDIM), HDIM)
+            qu = rq[at]
+            gu = rg[at]
             top = None
             for i in range(BALLS + BITS):
                 s = mm(keys_of(i), qu, NT)
                 if i >= BALLS:
-                    s = s + bias[i - BALLS, 0:1, qb * QB : (qb + 1) * QB]
+                    s = s + bias[i - BALLS, 0:1, some]
                 s_scr[i] = s
                 m = jnp.max(s.reshape(BALL // 8, 8, QB), axis=0)
                 top = m if top is None else jnp.maximum(top, m)
             top = jnp.max(top, axis=0, keepdims=True)
             total = jnp.zeros((8, QB), jnp.float32)
-            mean = jnp.zeros((8, QB), jnp.float32)
             for i in range(BALLS + BITS):
                 dp = mm(values_of(i), gu, NT)
                 e = jnp.exp(s_scr[i] - top)
                 s_scr[i] = e
                 dp_scr[i] = dp
                 total = total + jnp.sum(e.reshape(BALL // 8, 8, QB), axis=0)
-                mean = mean + jnp.sum((e * dp).reshape(BALL // 8, 8, QB), axis=0)
             scale = 1.0 / jnp.sum(total, axis=0, keepdims=True)
-            delta = jnp.sum(mean, axis=0, keepdims=True) * scale
-            at = slice(u * QB, (u + 1) * QB)
-            for i in range(BALLS + BITS):
-                pr = s_scr[i] * scale
-                ds = pr * (dp_scr[i] - delta)
-                p_scr[i * BALL : (i + 1) * BALL, at] = pr.astype(jnp.bfloat16)
+            mean = jnp.zeros((8, QB), jnp.float32)
+            for i in range(BALLS + BITS):
+                pb = (s_scr[i] * scale).astype(jnp.bfloat16)
+                p_scr[i * BALL : (i + 1) * BALL, at] = pb
+                part = pb.astype(jnp.float32) * dp_scr[i]
+                mean = mean + jnp.sum(part.reshape(BALL // 8, 8, QB), axis=0)
+            delta = jnp.sum(mean, axis=0, keepdims=True)
+            for i in range(BALLS + BITS):
+                ds = s_scr[i] * scale * (dp_scr[i] - delta)
                 ds_scr[i * BALL : (i + 1) * BALL, at] = ds.astype(jnp.bfloat16)
+            dqt[head, some] = mm(kt[head], ds_scr[:, at], NN)
 
         for b in range(BITS):
             at = slice(ROWS + b * BALL, ROWS + (b + 1) * BALL)
@@ -182,11 +191,6 @@
             at = slice(i * BALL, (i + 1) * BALL)
             gk[p, i] = mm(ds_scr[at], rq[...], NN)
             gv[p, i] = mm(p_scr[at], rg[...], NN)
-        for u in range(UNITS):
-            hh, qb = u // (ROWS // QB), u % (ROWS // QB)
-            dqt[hh * HDIM : (hh + 1) * HDIM, qb * QB : (qb + 1) * QB] = mm(
-                kt[hh * HDIM : (hh + 1) * HDIM], ds_scr[:, u * QB : (u + 1) * QB], NN
-            )
         for i in range(BALLS):
             dq = dqt[:, i * BALL : (i + 1) * BALL].T * HDIM**-0.5
             out[0, i, :, cols] = dq.astype(jnp.bfloat16)

time: 57.4 us -> 57.4 us (level)
  no operation moved by 1% of the time
where the time goes in v2:
time: 57.4 us; the launch traced here: 57.3 us
  Pallas kernels  56.7 us (99%)
  between operations  0.64 us (1%)
    pallas_call x1, Pallas kernels, body(): pl.pallas_call(kernel, out_shape=pltpu.VMEM((3, BALLS, BALL, WIDTH), jnp....  55.4 us
    pallas_call x1, Pallas kernels, body(): pl.pallas_call(deliver, out_shape=(balls, balls, balls), in_specs=[vmem],...  1.23 us

profile of v2, /device:TPU:8, one launch (start us, length us, event | category | flops | bytes accessed | tf_op | source)
XLA Modules:
  0.0 57.3 jit_solution(1097421095275077626)
XLA Ops:
  0.6 55.4 %shard_map.76.grads = bf16[3,4,128,512]{3,2,1,0:T(8,128)(2,1)S(1)} custom-call(s32[4,128]{1,0:T(4,128)} %bitcast.12, bf16[4,128,512]{2,1,0:T(8,128)(2,1)} %bitcast.8, bf16[4,128,512]{2,1,0:T(8,128)(2,1)} %bitcast.9, bf16[4,128,512]{2,1,0:T(8,128)(2,1)} %bitcast.10, bf16[4,128,512]{2,1,0:T(8,128)(2,1)} %bitcast.11), custom_call_target="tpu_custom_call" | custom-call | tf_op jit(solution)/shard_map/pallas_call | solution.py:243
  56.1 1.2 %shard_map.77 = (bf16[4,128,512]{2,1,0:T(8,128)(2,1)}, bf16[4,128,512]{2,1,0:T(8,128)(2,1)}, bf16[4,128,512]{2,1,0:T(8,128)(2,1)}) custom-call(bf16[3,4,128,512]{3,2,1,0:T(8,128)(2,1)S(1)} %shard_map.76.grads), custom_call_target="tpu_custom_call" | custom-call | tf_op jit(solution)/shard_map/pallas_call | solution.py:278

commit v3 on v2

--- a/solution.py
+++ b/solution.py
@@ -52,6 +52,7 @@
             copy.start()
     region = lax.axis_index("region")
     me = lax.axis_index("sub")
+    deep = me // 4
     peers = [jnp.bitwise_xor(me, 1 << b) for b in range(BITS)]
     barrier = pltpu.get_barrier_semaphore()
     for peer in peers:
@@ -101,12 +102,50 @@
             device_id_type=MESH,
         )
 
+    def give_near(p):
+        for b in (3, 2):
+
+            @pl.when(deep // (1 << (b - 2)) % 2 == 1)
+            def _():
+                back(p, b).start()
+
+        for b in (1, 0):
+            back(p, b).start()
+        for b in (2, 3):
+
+            @pl.when(deep // (1 << (b - 2)) % 2 == 0)
+            def _():
+                back(p, b).start()
+
+    def give_late(p):
+        @pl.when(deep < 4)
+        def _():
+            back(p, 4).start()
+
+        @pl.when(deep >= 4)
+        def _():
+            give_near(p)
+
+    def serve(p, copy, bits):
+        for b in (4, 3, 2):
+
+            @pl.when(deep // (1 << (b - 2)) % 2 == 1)
+            def _():
+                copy(p, b).start()
+
+        for b in bits:
+            copy(p, b).start()
+        for b in (2, 3, 4):
+
+            @pl.when(deep // (1 << (b - 2)) % 2 == 0)
+            def _():
+                copy(p, b).start()
+
     pl.semaphore_wait(barrier, BITS)
 
     @pl.loop(0, PAIRS)
     def _(p):
-        for b in SENDS:
-            ahead(p, b).start()
+        serve(p, ahead, (1, 0))
 
     for b in range(BITS):
         for r in range(BALLS):
@@ -185,8 +224,22 @@
             at = slice(ROWS + b * BALL, ROWS + (b + 1) * BALL)
             bsend[p, 0, b] = mm(ds_scr[at], rq[...], NN).astype(jnp.bfloat16)
             bsend[p, 1, b] = mm(p_scr[at], rg[...], NN).astype(jnp.bfloat16)
-        for b in SENDS:
-            back(p, b).start()
+        @pl.when(deep < 4)
+        def _():
+            give_near(p)
+
+        @pl.when(deep >= 4)
+        def _():
+            back(p, 4).start()
+
+        @pl.when(p > 0)
+        def _():
+            give_late(p - 1)
+
+        @pl.when(p == PAIRS - 1)
+        def _():
+            give_late(p)
+
         for i in range(BALLS):
             at = slice(i * BALL, (i + 1) * BALL)
             gk[p, i] = mm(ds_scr[at], rq[...], NN)

time: 57.4 us -> 55.3 us (0.963)
  Pallas kernels: 56.7 us -> 54.4 us
    pallas_call x1, Pallas kernels: 55.4 us -> 53.1 us  [body(): pl.pallas_call(kernel, out_shape=pltpu.VMEM((3, BALLS, BALL, WIDTH), jnp....]
where the time goes in v3:
time: 55.3 us; the launch traced here: 55 us
  Pallas kernels  54.4 us (98%)
  between operations  0.64 us (1%)
    pallas_call x1, Pallas kernels, body(): pl.pallas_call(kernel, out_shape=pltpu.VMEM((3, BALLS, BALL, WIDTH), jnp....  53.1 us
    pallas_call x1, Pallas kernels, body(): pl.pallas_call(deliver, out_shape=(balls, balls, balls), in_specs=[vmem],...  1.23 us

profile of v3, /device:TPU:8, one launch (start us, length us, event | category | flops | bytes accessed | tf_op | source)
XLA Modules:
  0.0 55.0 jit_solution(3381642948175448739)
XLA Ops:
  0.6 53.1 %shard_map.76.grads = bf16[3,4,128,512]{3,2,1,0:T(8,128)(2,1)S(1)} custom-call(s32[4,128]{1,0:T(4,128)} %bitcast.12, bf16[4,128,512]{2,1,0:T(8,128)(2,1)} %bitcast.8, bf16[4,128,512]{2,1,0:T(8,128)(2,1)} %bitcast.9, bf16[4,128,512]{2,1,0:T(8,128)(2,1)} %bitcast.10, bf16[4,128,512]{2,1,0:T(8,128)(2,1)} %bitcast.11), custom_call_target="tpu_custom_call" | custom-call | tf_op jit(solution)/shard_map/pallas_call | solution.py:296
  53.8 1.2 %shard_map.77 = (bf16[4,128,512]{2,1,0:T(8,128)(2,1)}, bf16[4,128,512]{2,1,0:T(8,128)(2,1)}, bf16[4,128,512]{2,1,0:T(8,128)(2,1)}) custom-call(bf16[3,4,128,512]{3,2,1,0:T(8,128)(2,1)S(1)} %shard_map.76.grads), custom_call_target="tpu_custom_call" | custom-call | tf_op jit(solution)/shard_map/pallas_call | solution.py:331

commit v4 on v3

--- a/solution.py
+++ b/solution.py
@@ -126,26 +126,12 @@
         def _():
             give_near(p)
 
-    def serve(p, copy, bits):
-        for b in (4, 3, 2):
-
-            @pl.when(deep // (1 << (b - 2)) % 2 == 1)
-            def _():
-                copy(p, b).start()
-
-        for b in bits:
-            copy(p, b).start()
-        for b in (2, 3, 4):
-
-            @pl.when(deep // (1 << (b - 2)) % 2 == 0)
-            def _():
-                copy(p, b).start()
-
     pl.semaphore_wait(barrier, BITS)
 
     @pl.loop(0, PAIRS)
     def _(p):
-        serve(p, ahead, (1, 0))
+        for b in SENDS:
+            ahead(p, b).start()
 
     for b in range(BITS):
         for r in range(BALLS):
@@ -256,13 +242,20 @@
     @pl.loop(0, PAIRS)
     def _(p):
         cols = pl.ds(pl.multiple_of(p * SLAB, SLAB), SLAB)
-        for b in range(BITS):
-            back(p, b).wait_recv()
+        for bits in ((0, 1, 2), (3,)):
+            for b in bits:
+                back(p, b).wait_recv()
+            for i in range(BALLS):
+                ak, av = gk[p, i], gv[p, i]
+                for b in bits:
+                    ak = ak + share[i][b] * brecv[p, 0, b].astype(jnp.float32)
+                    av = av + share[i][b] * brecv[p, 1, b].astype(jnp.float32)
+                gk[p, i] = ak
+                gv[p, i] = av
+        back(p, 4).wait_recv()
         for i in range(BALLS):
-            ak, av = gk[p, i], gv[p, i]
-            for b in range(BITS):
-                ak = ak + share[i][b] * brecv[p, 0, b].astype(jnp.float32)
-                av = av + share[i][b] * brecv[p, 1, b].astype(jnp.float32)
+            ak = gk[p, i] + share[i][4] * brecv[p, 0, 4].astype(jnp.float32)
+            av = gv[p, i] + share[i][4] * brecv[p, 1, 4].astype(jnp.float32)
             out[1, i, :, cols] = ak.astype(jnp.bfloat16)
             out[2, i, :, cols] = av.astype(jnp.bfloat16)
 

time: 55.3 us -> 55.2 us (level)
  no operation moved by 1% of the time
where the time goes in v4:
time: 55.2 us; the launch traced here: 55.1 us
  Pallas kernels  54.5 us (99%)
  between operations  0.64 us (1%)
    pallas_call x1, Pallas kernels, body(): pl.pallas_call(kernel, out_shape=pltpu.VMEM((3, BALLS, BALL, WIDTH), jnp....  53.2 us
    pallas_call x1, Pallas kernels, body(): pl.pallas_call(deliver, out_shape=(balls, balls, balls), in_specs=[vmem],...  1.23 us

profile of v4, /device:TPU:8, one launch (start us, length us, event | category | flops | bytes accessed | tf_op | source)
XLA Modules:
  0.0 55.1 jit_solution(10293670062665749583)
XLA Ops:
  0.6 53.2 %shard_map.76.grads = bf16[3,4,128,512]{3,2,1,0:T(8,128)(2,1)S(1)} custom-call(s32[4,128]{1,0:T(4,128)} %bitcast.12, bf16[4,128,512]{2,1,0:T(8,128)(2,1)} %bitcast.8, bf16[4,128,512]{2,1,0:T(8,128)(2,1)} %bitcast.9, bf16[4,128,512]{2,1,0:T(8,128)(2,1)} %bitcast.10, bf16[4,128,512]{2,1,0:T(8,128)(2,1)} %bitcast.11), custom_call_target="tpu_custom_call" | custom-call | tf_op jit(solution)/shard_map/pallas_call | solution.py:289
  53.9 1.2 %shard_map.77 = (bf16[4,128,512]{2,1,0:T(8,128)(2,1)}, bf16[4,128,512]{2,1,0:T(8,128)(2,1)}, bf16[4,128,512]{2,1,0:T(8,128)(2,1)}) custom-call(bf16[3,4,128,512]{3,2,1,0:T(8,128)(2,1)S(1)} %shard_map.76.grads), custom_call_target="tpu_custom_call" | custom-call | tf_op jit(solution)/shard_map/pallas_call | solution.py:324
